TPU v7x, 128 devices: a whole 4x4x4 slice. The times are simulated.
128 devices in a mesh: dom: 64 (over z, y, x), sub: 2 (over core).
Axes of the slice: x: 4, y: 4, z: 4, core: 2. Of those that a mesh axis runs over, the one named last changes fastest.
Arguments:
- voltages: float32 [64, 4096], P(None, ('dom', 'sub')), may hold values from -6 to 6
- newton_steps: float32 [2, 64, 4096], P(None, None, ('dom', 'sub')), may hold values from -3 to 3
- cap_diag: float32 [64, 4096], P(None, ('dom', 'sub')), may hold values from 1 to 10
- preconditioner: float32 [64, 64, 4096], P(None, None, ('dom', 'sub')), may hold values from -0.75 to 0.75
- couple_block: int32 [8192], P(('dom', 'sub')), may hold values from 0 to 31
- couple_owner: int32 [8192, 1], P(('dom', 'sub')), may hold values from 0 to 127; in each aligned block of 64 rows (0 to 63, 64 to 127, ...) at most 2 rows name the same one
- couple_offset: int32 [8192], P(('dom', 'sub')), may hold values from 0 to 31
- couple_source: int32 [8192, 768], P(('dom', 'sub')), may hold values from 0 to 63
- couple_target: int32 [8192, 768], P(('dom', 'sub')), may hold values from 0 to 63
- couple_gain: float32 [8192, 768], P(('dom', 'sub')), may hold values from 0.05 to 0.5
- inner_source: int32 [4096, 768], P(('dom', 'sub')), may hold values from 0 to 63
- inner_target: int32 [4096, 768], P(('dom', 'sub')), may hold values from 0 to 63
- inner_gain: float32 [4096, 768], P(('dom', 'sub')), may hold values from 0.05 to 0.5
Outputs:
- preconditioned: float32 [2, 64, 4096], P(None, None, ('dom', 'sub'))
Inputs may be any that keep to these rules, and one draw needn't show every extreme that they name: `couple_owner`: within the 64 stamp blocks of one device no owner is named more than 2 times, a bound that some block reaches.
All inputs are finite; a program needn't handle non-finite values.
Results may differ from a plain program's by a relative error of at most 0.0041.
Values may be sent and summed in bfloat16 or wider, within the bound.
A program may use at most 64 MiB of HBM per device.

v0:
```python
import math

import jax
import jax.numpy as jnp
from jax import lax
from jax.sharding import PartitionSpec as P

BS = 64
NEWTON = 2


def conductance(gain, first, second):
    drop = first - second
    return (gain / (1.0 + drop * drop)).astype(jnp.bfloat16)


def couple_blocks(source, target, weight):
    row_count = source.shape[0]
    group_size = math.gcd(row_count, 32)
    node_ids = jnp.arange(BS, dtype=jnp.int32)

    def couple_one_group(pieces):
        group_source, group_target, group_weight = pieces
        hot_source = (group_source[..., None] == node_ids).astype(jnp.bfloat16)
        hot_target = (group_target[..., None] == node_ids).astype(jnp.bfloat16) * (-group_weight)[
            ..., None
        ]
        return jnp.einsum(
            "gkj,gki->gji", hot_target, hot_source, preferred_element_type=jnp.float32
        ).astype(jnp.bfloat16)

    shaped = tuple(
        (
            item.reshape(row_count // group_size, group_size, item.shape[1])
            for item in (source, target, weight)
        )
    )
    stacked = lax.map(couple_one_group, shaped)
    return stacked.reshape(row_count, BS, BS)


def inner_images(field, update, capacity, source, target, gain):
    row_count = source.shape[0]
    group_size = math.gcd(row_count, 32)
    node_ids = jnp.arange(BS, dtype=jnp.int32)
    by_block = field.T
    weight = conductance(
        gain,
        jnp.take_along_axis(by_block, source, axis=1),
        jnp.take_along_axis(by_block, target, axis=1),
    )
    identity = jnp.eye(BS, dtype=jnp.float32)

    def inner_one_group(pieces):
        group_source, group_target, group_weight, group_capacity, group_update = pieces
        difference = (group_source[..., None] == node_ids).astype(jnp.bfloat16) - (
            group_target[..., None] == node_ids
        ).astype(jnp.bfloat16)
        weighted = difference * group_weight[..., None]
        matrix = jnp.einsum(
            "gki,gkj->gij", weighted, difference, preferred_element_type=jnp.float32
        )
        matrix = (matrix + group_capacity[:, :, None] * identity[None]).astype(jnp.bfloat16)
        return jnp.einsum("gij,gj->gi", matrix, group_update, preferred_element_type=jnp.float32)

    pieces = (source, target, weight, capacity.T, update.T)
    shaped = tuple(
        (item.reshape((row_count // group_size, group_size) + item.shape[1:]) for item in pieces)
    )
    stacked = lax.map(inner_one_group, shaped)
    return stacked.reshape(row_count, BS).T


def per_device(
    voltages,
    newton_steps,
    cap_diag,
    preconditioner,
    couple_block,
    couple_owner,
    couple_offset,
    couple_source,
    couple_target,
    couple_gain,
    inner_source,
    inner_target,
    inner_gain,
):
    devices_all = lax.axis_size(("dom", "sub"))
    stamp_count = couple_block.shape[0]
    block_count = voltages.shape[1]
    per_owner = max(2, 2 * stamp_count // devices_all)
    slot_total = devices_all * per_owner
    owners = couple_owner[:, 0]
    position = jnp.arange(stamp_count, dtype=jnp.int32)
    earlier = (owners[:, None] == owners[None, :]) & (position[None, :] < position[:, None])
    slot_index = owners * per_owner + jnp.sum(earlier, axis=1, dtype=jnp.int32)
    requests = jnp.full((slot_total,), -1, jnp.int32).at[slot_index].set(couple_offset)
    asked = lax.all_to_all(requests, ("dom", "sub"), split_axis=0, concat_axis=0, tiled=True)
    row_onehot = (asked[:, None] == jnp.arange(block_count, dtype=jnp.int32)[None, :]).astype(
        jnp.float32
    )
    asked_block = jnp.maximum(asked, 0)
    field = voltages
    results = []
    for newton in range(NEWTON):
        update = newton_steps[newton].astype(jnp.bfloat16)
        sent_field = field[:, asked_block]
        remote_field = lax.all_to_all(
            sent_field.astype(jnp.bfloat16), ("dom", "sub"), split_axis=1, concat_axis=1, tiled=True
        ).astype(sent_field.dtype)
        inner_part = inner_images(field, update, cap_diag, inner_source, inner_target, inner_gain)
        by_block = field.T
        local_rows = jnp.take_along_axis(by_block[couple_block], couple_source, axis=1)
        remote_rows = jnp.take_along_axis(remote_field.T[slot_index], couple_target, axis=1)
        couple_weight = conductance(couple_gain, local_rows, remote_rows)
        matrices = couple_blocks(couple_source, couple_target, couple_weight)
        local_update = update.T[couple_block]
        local_images = jnp.einsum(
            "sji,si->sj", matrices, local_update, preferred_element_type=jnp.float32
        )
        image_buffer = jnp.zeros((slot_total, BS), jnp.float32).at[slot_index].set(local_images)
        images = lax.all_to_all(
            image_buffer.astype(jnp.bfloat16),
            ("dom", "sub"),
            split_axis=0,
            concat_axis=0,
            tiled=True,
        ).astype(image_buffer.dtype)
        couple_part = jnp.dot(images.T, row_onehot, precision=lax.Precision.HIGHEST)
        total = inner_part + couple_part
        results.append(
            jnp.einsum("ijr,jr->ir", preconditioner, total, precision=lax.Precision.HIGHEST)
        )
        field = field + newton_steps[newton]
    return jnp.stack(results)


def solution(mesh):
    in_specs = (
        P(None, ("dom", "sub")),
        P(None, None, ("dom", "sub")),
        P(None, ("dom", "sub")),
        P(None, None, ("dom", "sub")),
        P(("dom", "sub")),
        P(("dom", "sub"), None),
        P(("dom", "sub")),
        P(("dom", "sub"), None),
        P(("dom", "sub"), None),
        P(("dom", "sub"), None),
        P(("dom", "sub"), None),
        P(("dom", "sub"), None),
        P(("dom", "sub"), None),
    )
    out_specs = P(None, None, ("dom", "sub"))
    return jax.shard_map(
        per_device, mesh=mesh, in_specs=in_specs, out_specs=out_specs, check_vma=False
    )
```

profile of v0, /device:TPU:1, one launch (start us, length us, event | category | flops | bytes accessed | tf_op | source)
XLA Modules:
  0.0 1987.0 jit_solution(867388449065161821)
XLA Ops:
  3.3 11.5 all-to-all-start
  14.7 0.9 bitcast_or_fusion.2
  15.7 0.9 bitcast_or_fusion.3
  16.7 157.6 %gather_fusion.9 = f32[24576]{0:T(1024)S(1)} fusion(f32[32,64]{1,0:T(8,128)S(1)} %bitcast.147, s32[24576]{0:T(1024)S(1)} %reshape.341), kind=kCustom, calls=%fused_computation.2.clone | custom fusion | bytes 393216 | tf_op jit(solution)/shard_map/jit(take_along_axis)/gather | solution.py:50
  174.2 157.6 %gather_fusion.8 = f32[24576]{0:T(1024)S(1)} fusion(f32[32,64]{1,0:T(8,128)S(1)} %bitcast.148, s32[24576]{0:T(1024)S(1)} %reshape.336), kind=kCustom, calls=%fused_computation.clone | custom fusion | bytes 393216 | tf_op jit(solution)/shard_map/jit(take_along_axis)/gather | solution.py:49
  331.8 157.6 %gather_fusion.13 = f32[24576]{0:T(1024)S(1)} fusion(f32[32,64]{1,0:T(8,128)S(1)} %bitcast.150, s32[24576]{0:T(1024)S(1)} %reshape.341), kind=kCustom, calls=%fused_computation.4.clone | custom fusion | bytes 393216 | tf_op jit(solution)/shard_map/jit(take_along_axis)/gather | solution.py:50
  489.4 157.6 %gather_fusion.12 = f32[24576]{0:T(1024)S(1)} fusion(f32[32,64]{1,0:T(8,128)S(1)} %bitcast.151, s32[24576]{0:T(1024)S(1)} %reshape.336), kind=kCustom, calls=%fused_computation.3.clone | custom fusion | bytes 393216 | tf_op jit(solution)/shard_map/jit(take_along_axis)/gather | solution.py:49
  648.3 2.9 fusion.73
  651.2 2.9 fusion.78
  655.7 1.3 gather_fusion.1
  657.0 9.8 all-to-all-start.1
  668.0 314.6 %gather_fusion.10 = f32[49152]{0:T(1024)S(1)} fusion(f32[64,64]{1,0:T(8,128)S(1)} %gather_fusion, s32[49152]{0:T(1024)S(1)} %reshape.346), kind=kCustom, calls=%fused_computation.1.clone | custom fusion | bytes 786432 | tf_op jit(solution)/shard_map/jit(take_along_axis)/gather | solution.py:114
  983.4 314.6 %gather_fusion.14 = f32[49152]{0:T(1024)S(1)} fusion(f32[64,64]{1,0:T(8,128)S(1)} %gather_fusion.4, s32[49152]{0:T(1024)S(1)} %reshape.346), kind=kCustom, calls=%fused_computation.6.clone | custom fusion | bytes 786432 | tf_op jit(solution)/shard_map/jit(take_along_axis)/gather | solution.py:114
  1298.7 1.6 copy.21
  1300.3 1.2 gather_fusion.3
  1301.5 1.3 gather_fusion.5
  1303.6 9.8 all-to-all-start.3
  1314.0 314.6 %gather_fusion.11 = f32[49152]{0:T(1024)S(1)} fusion(f32[64,64]{1,0:T(8,128)S(1)} %gather_fusion.2, s32[49152]{0:T(1024)S(1)} %reshape.351), kind=kCustom, calls=%fused_computation.5.clone | custom fusion | bytes 786432 | tf_op jit(solution)/shard_map/jit(take_along_axis)/gather | solution.py:115
  1629.3 314.6 %gather_fusion.15 = f32[49152]{0:T(1024)S(1)} fusion(f32[64,64]{1,0:T(8,128)S(1)} %gather_fusion.6, s32[49152]{0:T(1024)S(1)} %reshape.351), kind=kCustom, calls=%fused_computation.7.clone | custom fusion | bytes 786432 | tf_op jit(solution)/shard_map/jit(take_along_axis)/gather | solution.py:115
  1944.5 3.3 while.33
  1944.6 1.6 fusion.140
  1946.2 1.6 fusion.140
  1950.0 9.8 all-to-all-start.4
  1960.0 3.3 while.32
  1960.1 1.6 fusion.138
  1961.7 1.6 fusion.138
  1964.0 1.1 scatter_custom_fusion.1
  1965.7 3.7 all-to-all-done.4
  1969.4 6.1 all-to-all-start.2
  1975.8 1.0 fusion.124
  1976.7 8.4 all-to-all-done.2
  1985.4 1.0 fusion.123
  (101 shorter events, 16.1 us)
Async XLA Ops:
  0.0 16.6 copy-start
  1.6 652.5 %copy-start.15 = (s32[64]{0:T(128)}, s32[64]{0:T(128)S(1)}, u32[]{:S(2)}) copy-start(s32[64]{0:T(128)S(1)} %fusion.119) | copy-start | bytes 772
  3.3 650.8 %all-to-all-start = ((s32[128,2,1]{1,2,0:T(1,128)}), s32[128,2,1]{1,2,0:T(1,128)S(1)}, u32[]{:S(2)}, u32[]{:S(2)}) async-start(s32[128,2,1]{1,2,0:T(1,128)} %bitcast.15), calls=%async_computation | async-start | bytes 131072 | tf_op jit(solution)/shard_map/all_to_all | solution.py:99
  174.2 157.6 %copy-start.12 = (f32[2,64,32]{1,2,0:T(8,128)S(1)}, f32[2,64,32]{1,2,0:T(8,128)}, u32[]{:S(2)}) copy-start(f32[2,64,32]{1,2,0:T(8,128)} %param.22) | copy-start | bytes 49156
  489.4 157.8 %copy-start.1 = (s32[64,768]{1,0:T(8,128)S(1)}, s32[64,768]{1,0:T(8,128)}, u32[]{:S(2)}) copy-start(s32[64,768]{1,0:T(8,128)} %param.29) | copy-start | bytes 589828
  647.0 0.7 copy-start.17
  647.0 0.9 copy-start.3
  647.0 1.0 copy-start.9
  647.0 1.0 copy-start.10
  647.0 1.1 copy-start.11
  647.2 1.1 copy-start.16
  657.0 646.6 %all-to-all-start.1 = ((bf16[64,128,2]{0,2,1:T(2,128)(2,1)}), bf16[64,128,2]{0,2,1:T(2,128)(2,1)S(1)}, u32[]{:S(2)}, u32[]{:S(2)}) async-start(bf16[64,128,2]{0,2,1:T(2,128)(2,1)} %bitcast.17), calls=%async_computation.1 | async-start | bytes 131072 | tf_op jit(solution)/shard_map/all_to_all | solution.py:109
  983.4 315.3 %copy-start.6 = (f32[64,64,32]{1,2,0:T(8,128)S(1)}, f32[64,64,32]{1,2,0:T(8,128)}, u32[]{:S(2)}) copy-start(f32[64,64,32]{1,2,0:T(8,128)} %param.24) | copy-start | bytes 1572868
  1303.6 325.0 %all-to-all-start.3 = ((bf16[64,128,2]{0,2,1:T(2,128)(2,1)}), bf16[64,128,2]{0,2,1:T(2,128)(2,1)S(1)}, u32[]{:S(2)}, u32[]{:S(2)}) async-start(bf16[64,128,2]{0,2,1:T(2,128)(2,1)} %bitcast.46), calls=%async_computation.3 | async-start | bytes 131072 | tf_op jit(solution)/shard_map/all_to_all | solution.py:109
  1629.2 314.7 %copy-start.2 = (s32[64,768]{1,0:T(8,128)S(1)}, s32[64,768]{1,0:T(8,128)}, u32[]{:S(2)}) copy-start(s32[64,768]{1,0:T(8,128)} %param.29) | copy-start | bytes 589828
  1629.2 314.7 %copy-start.4 = (s32[64,768]{1,0:T(8,128)S(1)}, s32[64,768]{1,0:T(8,128)}, u32[]{:S(2)}) copy-start(s32[64,768]{1,0:T(8,128)} %param.28) | copy-start | bytes 589828
  1629.3 314.7 %copy-start.7 = (f32[64,768]{1,0:T(8,128)S(1)}, f32[64,768]{1,0:T(8,128)}, u32[]{:S(2)}) copy-start(f32[64,768]{1,0:T(8,128)} %reshape.349) | copy-start | bytes 589828
  1629.3 314.7 %copy-start.8 = (f32[64,768]{1,0:T(8,128)S(1)}, f32[64,768]{1,0:T(8,128)}, u32[]{:S(2)}) copy-start(f32[64,768]{1,0:T(8,128)} %param.30) | copy-start | bytes 589828
  1950.0 19.4 all-to-all-start.4
  1960.0 3.4 copy-start.13
  1963.4 12.1 copy-start.14
  1963.4 12.1 copy-start.19
  1963.4 12.4 copy-start.5
  1964.0 21.1 %copy-start.18 = (f32[32,1,64]{2,1,0:T(1,128)S(1)}, f32[32,1,64]{2,1,0:T(1,128)}, u32[]{:S(2)}) copy-start(f32[32,1,64]{2,1,0:T(1,128)} %fusion.78) | copy-start | bytes 24580
  1969.4 15.7 all-to-all-start.2
where the time goes:
time: 1990 us
  local copies, waits for them, and re-layouts  1900 us (95%)
  starting transfers between devices  46.8 us (2%)
    gather x5, local copies, waits for them, and re-layouts, per_device(): jnp.take_along_axis(by_block[couple_block], couple_source, axis=1)  630 us
    gather x5, local copies, waits for them, and re-layouts, per_device(): jnp.take_along_axis(remote_field.T[slot_index], couple_target, axis=1)  629 us
    gather x5, local copies, waits for them, and re-layouts, inner_images(): jnp.take_along_axis(by_block, target, axis=1)  315 us
    gather x5, local copies, waits for them, and re-layouts, inner_images(): jnp.take_along_axis(by_block, source, axis=1)  315 us
  transfers between devices with their start and end apart: 5, of which 2 were waited for; matrix products, arithmetic and copies ran while one was open for 80% of the time, Pallas kernels for 0%

commit v1 on v0

v1 whole, which is shorter than its diff:
```python
import functools

import jax
import jax.numpy as jnp
from jax import lax
from jax.experimental import pallas as pl
from jax.experimental.pallas import tpu as pltpu
from jax.sharding import PartitionSpec as P

GROUP_A = 8
MESH = pl.DeviceIdType.MESH
F32 = jnp.float32
BF16 = jnp.bfloat16


def iota(shape, axis):
    return lax.broadcasted_iota(jnp.int32, shape, axis)


def lookup(table, index):
    pieces = [
        jnp.take_along_axis(table, index[:, at : at + 128], axis=1, mode="promise_in_bounds")
        for at in range(0, index.shape[1], 128)
    ]
    return jnp.concatenate(pieces, axis=1)


def conductance(gain, first, second):
    drop = first - second
    return (gain / (1.0 + drop * drop)).astype(BF16).astype(F32)


def two_parts(first, second):
    rows = []
    for item in (first, second):
        high = item.astype(BF16).astype(F32)
        rows += [high, item - high]
    return jnp.concatenate(rows, axis=0).astype(BF16)


def diagonal(product, nodes):
    row = iota((8, 128), 0)
    lane = iota((8, 128), 1)
    full = []
    for at in (0, 16):
        both = product[at : at + 8] + product[at + 8 : at + 16]
        total = None
        for c in range(4):
            piece = jnp.where(row == 2 * c + lane // nodes, both[:, 128 * c : 128 * c + 128], 0.0)
            total = piece if total is None else total + piece
        full.append(total + pltpu.roll(total, nodes, 1))
    return jnp.where(lane < nodes, full[0], full[1])


def nt_dot(left, right):
    return lax.dot_general(left, right, (((1,), (1,)), ((), ())), preferred_element_type=F32)


def body(
    sizes,
    volt_h,
    step_h,
    cap_h,
    pre_h,
    cblk_h,
    cown_h,
    coff_h,
    csrc_h,
    ctgt_h,
    cgain_h,
    isrc_h,
    itgt_h,
    igain_h,
    out,
    volt,
    step,
    cap,
    pre,
    cblk,
    cown,
    coff,
    csrc,
    ctgt,
    cgain,
    isrc,
    itgt,
    igain,
    table,
    update,
    col_table,
    col_update,
    far_table,
    image,
    inner,
    hot,
    hot_inner,
    near0,
    near1,
    upd0,
    upd1,
    slot_hot,
    slot_hot_t,
    gathered,
    req_send,
    req_recv,
    sel,
    sel_t,
    resp_send,
    resp_recv,
    img_send,
    img_recv,
    sum_send,
    sum_recv,
    in_sem,
    send_b,
    recv_b,
    send_a,
    recv_a,
):
    ga, gb, blocks, stamps, nodes, elements = sizes
    per = 2 * ga
    dev = lax.axis_index("dom") * 2 + lax.axis_index("sub")
    my_a = lax.rem(dev, ga)
    my_b = dev // ga

    def place(b, a):
        other = b * ga + a
        return (other // 2, lax.rem(other, 2))

    partners_a = [lax.rem(my_a + k, ga) for k in range(1, ga)]
    partners_b = [lax.rem(my_b + k, gb) for k in range(1, gb)]

    barrier = pltpu.get_barrier_semaphore()
    for b in partners_b:
        pl.semaphore_signal(barrier, inc=1, device_id=place(b, my_a), device_id_type=MESH)
    for a in partners_a:
        pl.semaphore_signal(barrier, inc=1, device_id=place(my_b, a), device_id_type=MESH)

    pairs = [
        (cown_h, cown),
        (coff_h, coff),
        (volt_h, volt),
        (step_h, step),
        (cblk_h, cblk),
        (cap_h, cap),
        (isrc_h, isrc),
        (itgt_h, itgt),
        (igain_h, igain),
        (csrc_h, csrc),
        (ctgt_h, ctgt),
        (cgain_h, cgain),
        (pre_h, pre),
    ]
    loads = [pltpu.make_async_copy(src, dst, in_sem.at[n]) for n, (src, dst) in enumerate(pairs)]
    for item in loads:
        item.start()
    for item in loads[:6]:
        item.wait()

    eye = iota((stamps, stamps), 0) == iota((stamps, stamps), 1)

    def column(row):
        spread = jnp.broadcast_to(row, (stamps, stamps))
        return jnp.sum(jnp.where(eye, spread, 0.0), axis=1, keepdims=True)

    own_row = cown[...].astype(F32)
    own_col = column(own_row)
    same = own_col == own_row
    before = iota((stamps, stamps), 0) < iota((stamps, stamps), 1)
    after = iota((stamps, stamps), 0) > iota((stamps, stamps), 1)
    slot_row = own_row * 2.0 + jnp.sum(jnp.where(same & before, 1.0, 0.0), axis=0, keepdims=True)
    slot_col = own_col * 2.0 + jnp.sum(jnp.where(same & after, 1.0, 0.0), axis=1, keepdims=True)
    slots = gb * per
    slot_hot[...] = jnp.where(iota((slots, stamps), 0).astype(F32) == slot_row, 1.0, 0.0).astype(BF16)
    slot_hot_t[...] = jnp.where(iota((stamps, slots), 1).astype(F32) == slot_col, 1.0, 0.0).astype(BF16)
    off_col = column(coff[...].astype(F32)) + 1.0
    asked = jnp.dot(
        slot_hot[...], jnp.broadcast_to(off_col, (stamps, 128)).astype(BF16), preferred_element_type=F32
    )
    owner_a = lax.rem(iota((slots, 128), 0), per) // 2
    asked = jnp.where(asked > 0.5, asked - 1.0 + (owner_a * blocks).astype(F32), -1.0)
    req_send[...] = asked.astype(BF16)

    v0 = volt[...]
    table[:, 0:nodes] = v0
    table[:, nodes : 2 * nodes] = v0 + step[0]
    update[:, 0:nodes] = step[0].astype(BF16).astype(F32)
    update[:, nodes : 2 * nodes] = step[1].astype(BF16).astype(F32)
    my_rows = pl.ds(pl.multiple_of(my_a * blocks, blocks), blocks)
    gathered[my_rows, :] = table[...].astype(BF16)

    pl.semaphore_wait(barrier, ga + gb - 2)

    def exchange_b(phase, source, target):
        copies = []
        for k, b in enumerate(partners_b):
            copies.append(
                pltpu.make_async_remote_copy(
                    src_ref=source.at[pl.ds(pl.multiple_of(b * per, per), per)],
                    dst_ref=target.at[pl.ds(pl.multiple_of(my_b * per, per), per)],
                    send_sem=send_b.at[phase, k],
                    recv_sem=recv_b.at[phase, k],
                    device_id=place(b, my_a),
                    device_id_type=MESH,
                )
            )
        for item in copies:
            item.start()
        mine = pl.ds(pl.multiple_of(my_b * per, per), per)
        target[mine, :] = source[mine, :]
        return copies

    requests = exchange_b(0, req_send, req_recv)
    tables = []
    for k, a in enumerate(partners_a):
        tables.append(
            pltpu.make_async_remote_copy(
                src_ref=gathered.at[my_rows],
                dst_ref=gathered.at[my_rows],
                send_sem=send_a.at[0, k],
                recv_sem=recv_a.at[0, k],
                device_id=place(my_b, a),
                device_id_type=MESH,
            )
        )
    for item in tables:
        item.start()

    blk_hot = jnp.where(
        iota((stamps, blocks), 1).astype(F32) == column(cblk[...].astype(F32)), 1.0, 0.0
    )
    col_table[...] = jnp.dot(
        blk_hot, table[...], precision=lax.Precision.HIGHEST, preferred_element_type=F32
    )
    col_update[...] = jnp.dot(
        blk_hot.astype(BF16), update[...].astype(BF16), preferred_element_type=F32
    )

    node = iota((nodes, elements), 0).astype(F32).astype(BF16)
    one = jnp.ones((nodes, elements), BF16)
    none = jnp.zeros((nodes, elements), BF16)

    def hot_rows(index):
        spread = jnp.broadcast_to(index.astype(F32), (nodes, elements)).astype(BF16)
        return jnp.where(spread == node, one, none)

    for item in loads[6:9]:
        item.wait()

    @pl.loop(0, blocks // 8)
    def _(g):
        rows = pl.ds(pl.multiple_of(g * 8, 8), 8)
        first, second, gain = isrc[rows, :], itgt[rows, :], igain[rows, :]
        tab, upd = table[rows, :], update[rows, :]
        weights = []
        for t in range(2):
            i, j = first + t * nodes, second + t * nodes
            g_t = conductance(gain, lookup(tab, i), lookup(tab, j))
            weights.append(g_t * (lookup(upd, i) - lookup(upd, j)))
        left = two_parts(*weights)
        for r in range(8):
            hot_inner[r * nodes : (r + 1) * nodes, :] = hot_rows(first[r : r + 1, :]) - hot_rows(
                second[r : r + 1, :]
            )
        spread = diagonal(nt_dot(left, hot_inner[...]), nodes)
        cap_here = cap[rows, :]
        inner[rows, :] = spread + jnp.concatenate([cap_here, cap_here], axis=1) * upd

    for item in requests:
        item.wait_recv()
    for item in tables:
        item.wait_recv()

    asked_here = req_recv[...].astype(F32)
    wide = ga * blocks
    for at in range(0, wide, 128):
        width = min(128, wide - at)
        lane = (iota((slots, width), 1) + at).astype(F32)
        sel[:, at : at + width] = jnp.where(asked_here[:, 0:width] == lane, 1.0, 0.0).astype(BF16)
    resp_send[...] = jnp.dot(sel[...], gathered[...], preferred_element_type=F32).astype(BF16)
    answers = exchange_b(1, resp_send, resp_recv)

    sel_t[...] = jnp.transpose(sel[...].astype(F32)).astype(BF16)

    for item in loads[9:12]:
        item.wait()

    @pl.loop(0, stamps // 8)
    def _(g):
        rows = pl.ds(pl.multiple_of(g * 8, 8), 8)
        first, second = csrc[rows, :], ctgt[rows, :]
        tab, upd = col_table[rows, :], col_update[rows, :]
        near0[rows, :] = lookup(tab, first)
        near1[rows, :] = lookup(tab, first + nodes)
        upd0[rows, :] = lookup(upd, first)
        upd1[rows, :] = lookup(upd, first + nodes)
        base = g * (8 * nodes)
        for r in range(8):
            hot[pl.ds(pl.multiple_of(base + r * nodes, nodes), nodes), :] = hot_rows(second[r : r + 1, :])

    for item in answers:
        item.wait_recv()
    far_table[...] = jnp.dot(slot_hot_t[...], resp_recv[...], preferred_element_type=F32)

    @pl.loop(0, stamps // 8)
    def _(g):
        rows = pl.ds(pl.multiple_of(g * 8, 8), 8)
        second, gain = ctgt[rows, :], cgain[rows, :]
        tab = far_table[rows, :]
        w0 = -conductance(gain, near0[rows, :], lookup(tab, second)) * upd0[rows, :]
        w1 = -conductance(gain, near1[rows, :], lookup(tab, second + nodes)) * upd1[rows, :]
        mine = hot[pl.ds(pl.multiple_of(g * (8 * nodes), 8 * nodes), 8 * nodes), :]
        image[rows, :] = diagonal(nt_dot(two_parts(w0, w1), mine), nodes)

    img_send[...] = jnp.dot(
        slot_hot[...], image[...].astype(BF16), preferred_element_type=F32
    ).astype(BF16)
    images = exchange_b(2, img_send, img_recv)
    loads[12].wait()
    for item in images:
        item.wait_recv()

    sum_send[...] = jnp.dot(sel_t[...], img_recv[...], preferred_element_type=F32).astype(BF16)
    sums = []
    for k, a in enumerate(partners_a):
        sums.append(
            pltpu.make_async_remote_copy(
                src_ref=sum_send.at[pl.ds(pl.multiple_of(a * blocks, blocks), blocks)],
                dst_ref=sum_recv.at[my_rows],
                send_sem=send_a.at[1, k],
                recv_sem=recv_a.at[1, k],
                device_id=place(my_b, a),
                device_id_type=MESH,
            )
        )
    for item in sums:
        item.start()
    sum_recv[my_rows, :] = sum_send[my_rows, :]
    for item in sums:
        item.wait_recv()

    total = inner[...]
    for a in range(ga):
        total = total + sum_recv[a * blocks : (a + 1) * blocks, :].astype(F32)
    y0 = total[:, 0:nodes]
    y1 = total[:, nodes : 2 * nodes]
    lane = iota((blocks, nodes), 1)
    r0 = jnp.zeros((blocks, nodes), F32)
    r1 = jnp.zeros((blocks, nodes), F32)
    for i in range(nodes):
        p = pre[i]
        r0 = jnp.where(lane == i, jnp.sum(p * y0, axis=1, keepdims=True), r0)
        r1 = jnp.where(lane == i, jnp.sum(p * y1, axis=1, keepdims=True), r1)
    out[0] = r0
    out[1] = r1

    for item in requests + tables + answers + images + sums:
        item.wait_send()


def solution(mesh):
    devices = mesh.shape["dom"] * mesh.shape["sub"]
    ga = min(GROUP_A, devices // 2)
    gb = devices // ga

    def per_device(*arrays):
        volt, step, cap, pre, cblk, cown, coff, csrc, ctgt, cgain, isrc, itgt, igain = arrays
        nodes, blocks = volt.shape
        stamps, elements = csrc.shape
        slots, wide = 2 * devices, ga * blocks
        given = (
            volt.T,
            step.transpose(0, 2, 1),
            cap.T,
            pre.transpose(0, 2, 1),
            cblk.reshape(1, stamps),
            cown.reshape(1, stamps),
            coff.reshape(1, stamps),
            csrc,
            ctgt,
            cgain,
            isrc,
            itgt,
            igain,
        )
        vmem = pltpu.VMEM
        scratch = [vmem(item.shape, item.dtype) for item in given]
        scratch += [
            vmem((blocks, 128), F32),
            vmem((blocks, 128), F32),
            vmem((stamps, 128), F32),
            vmem((stamps, 128), F32),
            vmem((stamps, 128), F32),
            vmem((stamps, 128), F32),
            vmem((blocks, 128), F32),
            vmem((stamps * nodes, elements), BF16),
            vmem((8 * nodes, elements), BF16),
            vmem((stamps, elements), F32),
            vmem((stamps, elements), F32),
            vmem((stamps, elements), F32),
            vmem((stamps, elements), F32),
            vmem((slots, stamps), BF16),
            vmem((stamps, slots), BF16),
            vmem((wide, 128), BF16),
            vmem((slots, 128), BF16),
            vmem((slots, 128), BF16),
            vmem((slots, wide), BF16),
            vmem((wide, slots), BF16),
            vmem((slots, 128), BF16),
            vmem((slots, 128), BF16),
            vmem((slots, 128), BF16),
            vmem((slots, 128), BF16),
            vmem((wide, 128), BF16),
            vmem((wide, 128), BF16),
            pltpu.SemaphoreType.DMA((len(given),)),
            pltpu.SemaphoreType.DMA((3, gb - 1)),
            pltpu.SemaphoreType.DMA((3, gb - 1)),
            pltpu.SemaphoreType.DMA((2, ga - 1)),
            pltpu.SemaphoreType.DMA((2, ga - 1)),
        ]
        result = pl.pallas_call(
            functools.partial(body, (ga, gb, blocks, stamps, nodes, elements)),
            out_shape=jax.ShapeDtypeStruct((2, blocks, nodes), F32),
            in_specs=[pl.BlockSpec(memory_space=pl.ANY)] * len(given),
            out_specs=pl.BlockSpec(memory_space=pltpu.VMEM),
            scratch_shapes=scratch,
            compiler_params=pltpu.CompilerParams(
                collective_id=0, has_side_effects=True, vmem_limit_bytes=32 * 1024 * 1024
            ),
        )(*given)
        return result.transpose(0, 2, 1)

    both = ("dom", "sub")
    in_specs = (
        P(None, both),
        P(None, None, both),
        P(None, both),
        P(None, None, both),
        P(both),
        P(both, None),
        P(both),
    ) + (P(both, None),) * 6
    return jax.shard_map(
        per_device, mesh=mesh, in_specs=in_specs, out_specs=P(None, None, both), check_vma=False
    )
```

time: 1990 us -> 42.9 us (0.02)
  local copies, waits for them, and re-layouts: 1900 us -> 10.2 us
  starting transfers between devices: 46.8 us -> 0 us
  Pallas kernels: 0 us -> 32.2 us
    gather x28 -> x0, local copies, waits for them, and re-layouts: 1900 us -> none  [the longest x5 630 us: per_device(): jnp.take_along_axis(by_block[couple_block], couple_source, axis=1)]
    all_to_all x5 -> x0, starting transfers between devices: 46.8 us -> none  [the longest x2 19.5 us: per_device(): lax.all_to_all(sent_field.astype(jnp.bfloat16), ('dom', 'sub'), split_axi...]
    pallas_call x0 -> x1, Pallas kernels: none -> 32.2 us  [per_device(): pl.pallas_call(functools.partial(body, (ga, gb, blocks, stamps, nodes, el...]
  transfers between devices with their start and end apart: 5 -> 0, of which waited for: 2 -> 0; matrix products, arithmetic and copies ran while one was open for 80% -> 0% of each run, Pallas kernels for 0% -> 0%
where the time goes in v1:
time: 42.9 us; the launch traced here: 42.4 us
  Pallas kernels  32.2 us (75%)
  local copies, waits for them, and re-layouts  10.2 us (24%)
    pallas_call x1, Pallas kernels, per_device(): pl.pallas_call(functools.partial(body, (ga, gb, blocks, stamps, nodes, el...  32.2 us
    unnamed x27, local copies, waits for them, and re-layouts  10.2 us

profile of v1, /device:TPU:1, one launch (start us, length us, event | category | flops | bytes accessed | tf_op | source)
XLA Modules:
  0.0 42.4 jit_solution(2504846929443204570)
XLA Ops:
  0.0 0.0 copy-start.10
  0.0 0.0 copy-start.11
  0.0 0.0 copy-start.12
  0.0 0.6 %copy-done.10 = s32[64]{0:T(128)S(1)} copy-done((s32[64]{0:T(128)S(1)}, s32[64]{0:T(128)}, u32[]{:S(2)}) %copy-start.10) | copy-done | bytes 280
  0.7 0.0 copy-done.11
  0.7 0.0 copy-done.12
  0.7 0.0 copy-start
  0.7 1.2 %copy-done = f32[64,64,32]{1,2,0:T(8,128)S(1)} copy-done((f32[64,64,32]{1,2,0:T(8,128)S(1)}, f32[64,64,32]{1,2,0:T(8,128)}, u32[]{:S(2)}) %copy-start) | copy-done | bytes 524312
  1.9 0.0 copy-start.1
  1.9 0.9 %copy-done.1 = s32[64,768]{1,0:T(8,128)S(1)} copy-done((s32[64,768]{1,0:T(8,128)S(1)}, s32[64,768]{1,0:T(8,128)}, u32[]{:S(2)}) %copy-start.1) | copy-done | bytes 196632
  2.8 0.0 copy-start.2
  2.8 0.9 %copy-done.2 = s32[64,768]{1,0:T(8,128)S(1)} copy-done((s32[64,768]{1,0:T(8,128)S(1)}, s32[64,768]{1,0:T(8,128)}, u32[]{:S(2)}) %copy-start.2) | copy-done | bytes 196632
  3.8 0.0 copy-start.3
  3.8 0.9 %copy-done.3 = f32[64,768]{1,0:T(8,128)S(1)} copy-done((f32[64,768]{1,0:T(8,128)S(1)}, f32[64,768]{1,0:T(8,128)}, u32[]{:S(2)}) %copy-start.3) | copy-done | bytes 196632
  4.7 0.0 copy-start.4
  4.7 0.9 %copy-done.4 = s32[32,768]{1,0:T(8,128)S(1)} copy-done((s32[32,768]{1,0:T(8,128)S(1)}, s32[32,768]{1,0:T(8,128)}, u32[]{:S(2)}) %copy-start.4) | copy-done | bytes 98328
  5.6 0.0 copy-start.5
  5.6 0.9 %copy-done.5 = s32[32,768]{1,0:T(8,128)S(1)} copy-done((s32[32,768]{1,0:T(8,128)S(1)}, s32[32,768]{1,0:T(8,128)}, u32[]{:S(2)}) %copy-start.5) | copy-done | bytes 98328
  6.5 0.0 copy-start.6
  6.5 0.9 %copy-done.6 = f32[32,768]{1,0:T(8,128)S(1)} copy-done((f32[32,768]{1,0:T(8,128)S(1)}, f32[32,768]{1,0:T(8,128)}, u32[]{:S(2)}) %copy-start.6) | copy-done | bytes 98328
  7.4 0.0 copy-start.7
  7.4 0.8 %copy-done.7 = f32[2,64,32]{1,2,0:T(8,128)S(1)} copy-done((f32[2,64,32]{1,2,0:T(8,128)S(1)}, f32[2,64,32]{1,2,0:T(8,128)}, u32[]{:S(2)}) %copy-start.7) | copy-done | bytes 16408
  8.1 0.0 copy-start.8
  8.1 0.7 %copy-done.8 = f32[64,32]{0,1:T(8,128)S(1)} copy-done((f32[64,32]{0,1:T(8,128)S(1)}, f32[64,32]{0,1:T(8,128)}, u32[]{:S(2)}) %copy-start.8) | copy-done | bytes 8216
  8.9 0.0 copy-start.9
  8.9 0.7 %copy-done.9 = f32[64,32]{0,1:T(8,128)S(1)} copy-done((f32[64,32]{0,1:T(8,128)S(1)}, f32[64,32]{0,1:T(8,128)}, u32[]{:S(2)}) %copy-start.9) | copy-done | bytes 8216
  9.6 32.2 %shard_map.127 = f32[2,32,64]{2,1,0:T(8,128)S(1)} custom-call(f32[32,64]{1,0:T(8,128)S(1)} %bitcast.11, f32[2,32,64]{2,1,0:T(8,128)S(1)} %bitcast.10, f32[32,64]{1,0:T(8,128)S(1)} %bitcast.12, f32[64,32,64]{2,1,0:T(8,128)S(1)} %bitcast.8, s32[1,64]{1,0:T(1,128)S(1)} %bitcast.13, s32[1,64]{1,0:T(1,128)S(1)} %bitcast.14, s32[1,64]{1,0:T(1,128)S(1)} %bitcast.15, ...), custom_call_target="tpu_custom_call" | custom-call | tf_op jit(solution)/shard_map/pallas_call | solution.py:421
  41.8 0.6 %copy.15 = f32[2,64,32]{1,2,0:T(8,128)} copy(f32[2,64,32]{1,2,0:T(8,128)S(1)} %bitcast.9) | data formatting | bytes 32768
Async XLA Ops:
  0.0 0.7 %copy-start.10 = (s32[64]{0:T(128)S(1)}, s32[64]{0:T(128)}, u32[]{:S(2)}) copy-start(s32[64]{0:T(128)} %param.17) | copy-start | bytes 772
  0.0 0.7 %copy-start.11 = (s32[64,1]{0,1:T(1,128)S(1)}, s32[64,1]{0,1:T(1,128)}, u32[]{:S(2)}) copy-start(s32[64,1]{0,1:T(1,128)} %param.18) | copy-start | bytes 772
  0.0 0.7 %copy-start.12 = (s32[64]{0:T(128)S(1)}, s32[64]{0:T(128)}, u32[]{:S(2)}) copy-start(s32[64]{0:T(128)} %param.19) | copy-start | bytes 772
  0.7 1.2 %copy-start = (f32[64,64,32]{1,2,0:T(8,128)S(1)}, f32[64,64,32]{1,2,0:T(8,128)}, u32[]{:S(2)}) copy-start(f32[64,64,32]{1,2,0:T(8,128)} %param.16) | copy-start | bytes 1572868
  1.9 0.9 %copy-start.1 = (s32[64,768]{1,0:T(8,128)S(1)}, s32[64,768]{1,0:T(8,128)}, u32[]{:S(2)}) copy-start(s32[64,768]{1,0:T(8,128)} %csrc_h.1) | copy-start | bytes 589828
  2.8 0.9 %copy-start.2 = (s32[64,768]{1,0:T(8,128)S(1)}, s32[64,768]{1,0:T(8,128)}, u32[]{:S(2)}) copy-start(s32[64,768]{1,0:T(8,128)} %ctgt_h.1) | copy-start | bytes 589828
  3.8 0.9 %copy-start.3 = (f32[64,768]{1,0:T(8,128)S(1)}, f32[64,768]{1,0:T(8,128)}, u32[]{:S(2)}) copy-start(f32[64,768]{1,0:T(8,128)} %cgain_h.1) | copy-start | bytes 589828
  4.7 0.9 %copy-start.4 = (s32[32,768]{1,0:T(8,128)S(1)}, s32[32,768]{1,0:T(8,128)}, u32[]{:S(2)}) copy-start(s32[32,768]{1,0:T(8,128)} %isrc_h.1) | copy-start | bytes 294916
  5.6 0.9 %copy-start.5 = (s32[32,768]{1,0:T(8,128)S(1)}, s32[32,768]{1,0:T(8,128)}, u32[]{:S(2)}) copy-start(s32[32,768]{1,0:T(8,128)} %itgt_h.1) | copy-start | bytes 294916
  6.5 0.9 %copy-start.6 = (f32[32,768]{1,0:T(8,128)S(1)}, f32[32,768]{1,0:T(8,128)}, u32[]{:S(2)}) copy-start(f32[32,768]{1,0:T(8,128)} %igain_h.1) | copy-start | bytes 294916
  7.4 0.8 %copy-start.7 = (f32[2,64,32]{1,2,0:T(8,128)S(1)}, f32[2,64,32]{1,2,0:T(8,128)}, u32[]{:S(2)}) copy-start(f32[2,64,32]{1,2,0:T(8,128)} %param.14) | copy-start | bytes 49156
  8.1 0.7 %copy-start.8 = (f32[64,32]{0,1:T(8,128)S(1)}, f32[64,32]{0,1:T(8,128)}, u32[]{:S(2)}) copy-start(f32[64,32]{0,1:T(8,128)} %param.13) | copy-start | bytes 24580
  8.9 0.7 %copy-start.9 = (f32[64,32]{0,1:T(8,128)S(1)}, f32[64,32]{0,1:T(8,128)}, u32[]{:S(2)}) copy-start(f32[64,32]{0,1:T(8,128)} %param.15) | copy-start | bytes 24580

commit v2 on v1

--- a/solution.py
+++ b/solution.py
@@ -7,6 +7,7 @@
 from jax.experimental.pallas import tpu as pltpu
 from jax.sharding import PartitionSpec as P
 
+DIGIT = 16
 GROUP_A = 8
 MESH = pl.DeviceIdType.MESH
 F32 = jnp.float32
@@ -94,6 +95,8 @@
     inner,
     hot,
     hot_inner,
+    pre_high,
+    pre_low,
     near0,
     near1,
     upd0,
@@ -130,12 +133,6 @@
     partners_a = [lax.rem(my_a + k, ga) for k in range(1, ga)]
     partners_b = [lax.rem(my_b + k, gb) for k in range(1, gb)]
 
-    barrier = pltpu.get_barrier_semaphore()
-    for b in partners_b:
-        pl.semaphore_signal(barrier, inc=1, device_id=place(b, my_a), device_id_type=MESH)
-    for a in partners_a:
-        pl.semaphore_signal(barrier, inc=1, device_id=place(my_b, a), device_id_type=MESH)
-
     pairs = [
         (cown_h, cown),
         (coff_h, coff),
@@ -154,6 +151,13 @@
     loads = [pltpu.make_async_copy(src, dst, in_sem.at[n]) for n, (src, dst) in enumerate(pairs)]
     for item in loads:
         item.start()
+
+    barrier = pltpu.get_barrier_semaphore()
+    for b in partners_b:
+        pl.semaphore_signal(barrier, inc=1, device_id=place(b, my_a), device_id_type=MESH)
+    for a in partners_a:
+        pl.semaphore_signal(barrier, inc=1, device_id=place(my_b, a), device_id_type=MESH)
+
     for item in loads[:6]:
         item.wait()
 
@@ -294,29 +298,59 @@
         near1[rows, :] = lookup(tab, first + nodes)
         upd0[rows, :] = lookup(upd, first)
         upd1[rows, :] = lookup(upd, first + nodes)
-        base = g * (8 * nodes)
+        low = second & (DIGIT - 1)
+        base = g * (8 * DIGIT)
         for r in range(8):
-            hot[pl.ds(pl.multiple_of(base + r * nodes, nodes), nodes), :] = hot_rows(second[r : r + 1, :])
+            spread = jnp.broadcast_to(low[r : r + 1, :].astype(F32), (DIGIT, elements)).astype(BF16)
+            hot[pl.ds(pl.multiple_of(base + r * DIGIT, DIGIT), DIGIT), :] = jnp.where(
+                spread == node[0:DIGIT], one[0:DIGIT], none[0:DIGIT]
+            )
 
     for item in answers:
         item.wait_recv()
     far_table[...] = jnp.dot(slot_hot_t[...], resp_recv[...], preferred_element_type=F32)
 
-    @pl.loop(0, stamps // 8)
+    @pl.loop(0, stamps // 8, unroll=True)
     def _(g):
         rows = pl.ds(pl.multiple_of(g * 8, 8), 8)
         second, gain = ctgt[rows, :], cgain[rows, :]
         tab = far_table[rows, :]
         w0 = -conductance(gain, near0[rows, :], lookup(tab, second)) * upd0[rows, :]
         w1 = -conductance(gain, near1[rows, :], lookup(tab, second + nodes)) * upd1[rows, :]
-        mine = hot[pl.ds(pl.multiple_of(g * (8 * nodes), 8 * nodes), 8 * nodes), :]
-        image[rows, :] = diagonal(nt_dot(two_parts(w0, w1), mine), nodes)
+        mine = hot[pl.ds(pl.multiple_of(g * (8 * DIGIT), 8 * DIGIT), 8 * DIGIT), :]
+        high = lax.shift_right_logical(second, DIGIT.bit_length() - 1)
+        parts = []
+        for item in (w0, w1):
+            upper = item.astype(BF16).astype(F32)
+            parts += [upper, item - upper]
+        left = [jnp.where(high == h, item, 0.0) for h in range(nodes // DIGIT) for item in parts]
+        spread = nt_dot(jnp.concatenate(left, axis=0).astype(BF16), mine)
+        lane = iota((8, 128), 1)
+        pick = iota((8, 128), 0) * DIGIT + (lane & (DIGIT - 1))
+        total = jnp.zeros((8, 128), F32)
+        for h in range(nodes // DIGIT):
+            for t in range(2):
+                at = (h * 4 + t * 2) * 8
+                piece = lookup(spread[at : at + 8] + spread[at + 8 : at + 16], pick)
+                total = jnp.where(lane // DIGIT == t * (nodes // DIGIT) + h, piece, total)
+        image[rows, :] = total
 
     img_send[...] = jnp.dot(
         slot_hot[...], image[...].astype(BF16), preferred_element_type=F32
     ).astype(BF16)
     images = exchange_b(2, img_send, img_recv)
     loads[12].wait()
+
+    @pl.loop(0, blocks // 2)
+    def _(c):
+        both = jnp.concatenate(
+            [pre[pl.ds(2 * c + n, nodes, stride=blocks), :] for n in range(2)], axis=1
+        )
+        upper = both.astype(BF16)
+        lanes = pl.ds(pl.multiple_of(c * 128, 128), 128)
+        pre_high[:, lanes] = upper
+        pre_low[:, lanes] = (both - upper.astype(F32)).astype(BF16)
+
     for item in images:
         item.wait_recv()
 
@@ -342,17 +376,22 @@
     total = inner[...]
     for a in range(ga):
         total = total + sum_recv[a * blocks : (a + 1) * blocks, :].astype(F32)
-    y0 = total[:, 0:nodes]
-    y1 = total[:, nodes : 2 * nodes]
-    lane = iota((blocks, nodes), 1)
-    r0 = jnp.zeros((blocks, nodes), F32)
-    r1 = jnp.zeros((blocks, nodes), F32)
-    for i in range(nodes):
-        p = pre[i]
-        r0 = jnp.where(lane == i, jnp.sum(p * y0, axis=1, keepdims=True), r0)
-        r1 = jnp.where(lane == i, jnp.sum(p * y1, axis=1, keepdims=True), r1)
-    out[0] = r0
-    out[1] = r1
+    width = 8 * nodes
+    keep = iota((8, width), 1) // nodes == iota((8, width), 0)
+    for at in range(0, blocks, 8):
+        here = total[at : at + 8]
+        turned = pltpu.roll(here, nodes, 1)
+        low_half = iota((8, 128), 1) < nodes
+        left = two_parts(
+            *(
+                jnp.where(keep, jnp.concatenate([item] * (width // 128), axis=1), 0.0)
+                for item in (jnp.where(low_half, here, turned), jnp.where(low_half, turned, here))
+            )
+        )
+        lanes = slice(at * nodes, (at + 8) * nodes)
+        result = nt_dot(left, pre_high[:, lanes]) + nt_dot(left, pre_low[:, lanes])
+        out[0, at : at + 8, :] = result[0:8] + result[8:16]
+        out[1, at : at + 8, :] = result[16:24] + result[24:32]
 
     for item in requests + tables + answers + images + sums:
         item.wait_send()
@@ -372,7 +411,7 @@
             volt.T,
             step.transpose(0, 2, 1),
             cap.T,
-            pre.transpose(0, 2, 1),
+            pre.transpose(0, 2, 1).reshape(nodes * blocks, nodes),
             cblk.reshape(1, stamps),
             cown.reshape(1, stamps),
             coff.reshape(1, stamps),
@@ -393,8 +432,10 @@
             vmem((stamps, 128), F32),
             vmem((stamps, 128), F32),
             vmem((blocks, 128), F32),
-            vmem((stamps * nodes, elements), BF16),
+            vmem((stamps * DIGIT, elements), BF16),
             vmem((8 * nodes, elements), BF16),
+            vmem((nodes, blocks * nodes), BF16),
+            vmem((nodes, blocks * nodes), BF16),
             vmem((stamps, elements), F32),
             vmem((stamps, elements), F32),
             vmem((stamps, elements), F32),
@@ -425,7 +466,7 @@
             out_specs=pl.BlockSpec(memory_space=pltpu.VMEM),
             scratch_shapes=scratch,
             compiler_params=pltpu.CompilerParams(
-                collective_id=0, has_side_effects=True, vmem_limit_bytes=32 * 1024 * 1024
+                collective_id=0, has_side_effects=True, vmem_limit_bytes=67043328
             ),
         )(*given)
         return result.transpose(0, 2, 1)

time: 42.9 us -> 31.3 us (0.73)
  local copies, waits for them, and re-layouts: 10.2 us -> 1.38 us
  Pallas kernels: 32.2 us -> 29.7 us
    unnamed x27 -> x1, local copies, waits for them, and re-layouts: 10.2 us -> 1.38 us
    pallas_call x1, Pallas kernels: 32.2 us -> 29.7 us  [per_device(): pl.pallas_call(functools.partial(body, (ga, gb, blocks, stamps, nodes, el...]
where the time goes in v2:
time: 31.3 us; the launch traced here: 31.1 us
  Pallas kernels  29.7 us (95%)
  local copies, waits for them, and re-layouts  1.38 us (4%)
    pallas_call x1, Pallas kernels, per_device(): pl.pallas_call(functools.partial(body, (ga, gb, blocks, stamps, nodes, el...  29.7 us
    unnamed x1, local copies, waits for them, and re-layouts  1.38 us

profile of v2, /device:TPU:1, one launch (start us, length us, event | category | flops | bytes accessed | tf_op | source)
XLA Modules:
  0.0 31.1 jit_solution(6662641628677683183)
XLA Ops:
  0.0 29.7 %shard_map.127 = f32[2,32,64]{2,1,0:T(8,128)} custom-call(f32[32,64]{1,0:T(8,128)} %bitcast.13, f32[2,32,64]{2,1,0:T(8,128)} %bitcast.12, f32[32,64]{1,0:T(8,128)} %bitcast.14, f32[2048,64]{1,0:T(8,128)} %bitcast.10, s32[1,64]{1,0:T(1,128)} %bitcast.15, s32[1,64]{1,0:T(1,128)} %bitcast.16, s32[1,64]{1,0:T(1,128)} %bitcast.17, s32[64,768]{1,0:T(8,128)} %csrc_h.1, ...), custom_call_target="tpu_custom_call" | custom-call | tf_op jit(solution)/shard_map/pallas_call | solution.py:462
  29.8 1.4 %copy.15 = f32[2,64,32]{1,2,0:T(8,128)} copy(f32[2,64,32]{1,2,0:T(8,128)} %bitcast.11) | data formatting | bytes 32768

commit v3 on v2

--- a/solution.py
+++ b/solution.py
@@ -107,31 +107,49 @@
     req_send,
     req_recv,
     sel,
-    sel_t,
     resp_send,
     resp_recv,
     img_send,
     img_recv,
-    sum_send,
-    sum_recv,
+    route_send,
+    route_recv,
     in_sem,
     send_b,
     recv_b,
     send_a,
     recv_a,
+    img_sem,
 ):
     ga, gb, blocks, stamps, nodes, elements = sizes
     per = 2 * ga
-    dev = lax.axis_index("dom") * 2 + lax.axis_index("sub")
-    my_a = lax.rem(dev, ga)
-    my_b = dev // ga
-
-    def place(b, a):
-        other = b * ga + a
-        return (other // 2, lax.rem(other, 2))
-
-    partners_a = [lax.rem(my_a + k, ga) for k in range(1, ga)]
-    partners_b = [lax.rem(my_b + k, gb) for k in range(1, gb)]
+    dom, core = lax.axis_index("dom"), lax.axis_index("sub")
+    my_z, my_y, my_x = dom // 16, lax.rem(dom // 4, 4), lax.rem(dom, 4)
+    my_q = lax.rem(my_x + 2 * my_y, 4)
+    my_a = my_y * 2 + core
+    my_b = my_z * 4 + my_q
+    flipped = my_y + 1 - 2 * lax.rem(my_y, 2)
+
+    def place(z, q, y, c):
+        return (z * 16 + y * 4 + lax.rem(q + 2 * y, 4), c)
+
+    def hops(dz, dq, dy):
+        return sum(min(d % 4, -d % 4) for d in (dz, dy, dq + 2 * dy))
+
+    partners_a = []
+    for k in range(1, ga):
+        a = lax.rem(my_a + k, ga)
+        partners_a.append((a, place(my_z, my_q, a // 2, lax.rem(a, 2))))
+    partners_b, partners = [], []
+    steps = [(dz, dq, dy, dc) for dz in range(gb // 4) for dq in range(4) for dy in range(4) for dc in range(2)]
+    for dz, dq, dy, dc in sorted(steps, key=lambda d: -hops(*d[:3])):
+        if (dz, dq, dy, dc) == (0, 0, 0, 0):
+            continue
+        z, q = lax.rem(my_z + dz, gb // 4), lax.rem(my_q + dq, 4)
+        y, c = lax.rem(my_y + dy, 4), lax.rem(core + dc, 2)
+        relay = (flipped if dq == 2 else my_y) * 2 + core
+        partners.append(((z * 4 + q) * ga + y * 2 + c, relay, place(z, q, y, c)))
+        if dc == 0 and dy == (1 if dq == 2 else 0):
+            partners_b.append((z * 4 + q, place(z, q, flipped if dq == 2 else my_y, core)))
 
     pairs = [
         (cown_h, cown),
@@ -153,10 +171,8 @@
         item.start()
 
     barrier = pltpu.get_barrier_semaphore()
-    for b in partners_b:
-        pl.semaphore_signal(barrier, inc=1, device_id=place(b, my_a), device_id_type=MESH)
-    for a in partners_a:
-        pl.semaphore_signal(barrier, inc=1, device_id=place(my_b, a), device_id_type=MESH)
+    for _, other in partners_b + partners_a:
+        pl.semaphore_signal(barrier, inc=1, device_id=other, device_id_type=MESH)
 
     for item in loads[:6]:
         item.wait()
@@ -172,8 +188,16 @@
     same = own_col == own_row
     before = iota((stamps, stamps), 0) < iota((stamps, stamps), 1)
     after = iota((stamps, stamps), 0) > iota((stamps, stamps), 1)
-    slot_row = own_row * 2.0 + jnp.sum(jnp.where(same & before, 1.0, 0.0), axis=0, keepdims=True)
-    slot_col = own_col * 2.0 + jnp.sum(jnp.where(same & after, 1.0, 0.0), axis=1, keepdims=True)
+
+    def renamed(owner):
+        y = lax.shift_right_logical(owner, 3) & 3
+        q = (lax.shift_right_logical(owner, 1) + 2 * y) & 3
+        return ((lax.shift_right_logical(owner, 5) * 4 + q) * ga + y * 2 + (owner & 1)).astype(F32)
+
+    group_row = renamed(cown[...])
+    group_col = column(group_row)
+    slot_row = group_row * 2.0 + jnp.sum(jnp.where(same & before, 1.0, 0.0), axis=0, keepdims=True)
+    slot_col = group_col * 2.0 + jnp.sum(jnp.where(same & after, 1.0, 0.0), axis=1, keepdims=True)
     slots = gb * per
     slot_hot[...] = jnp.where(iota((slots, stamps), 0).astype(F32) == slot_row, 1.0, 0.0).astype(BF16)
     slot_hot_t[...] = jnp.where(iota((stamps, slots), 1).astype(F32) == slot_col, 1.0, 0.0).astype(BF16)
@@ -197,14 +221,14 @@
 
     def exchange_b(phase, source, target):
         copies = []
-        for k, b in enumerate(partners_b):
+        for k, (b, other) in enumerate(partners_b):
             copies.append(
                 pltpu.make_async_remote_copy(
                     src_ref=source.at[pl.ds(pl.multiple_of(b * per, per), per)],
                     dst_ref=target.at[pl.ds(pl.multiple_of(my_b * per, per), per)],
                     send_sem=send_b.at[phase, k],
                     recv_sem=recv_b.at[phase, k],
-                    device_id=place(b, my_a),
+                    device_id=other,
                     device_id_type=MESH,
                 )
             )
@@ -216,14 +240,14 @@
 
     requests = exchange_b(0, req_send, req_recv)
     tables = []
-    for k, a in enumerate(partners_a):
+    for k, (a, other) in enumerate(partners_a):
         tables.append(
             pltpu.make_async_remote_copy(
                 src_ref=gathered.at[my_rows],
                 dst_ref=gathered.at[my_rows],
                 send_sem=send_a.at[0, k],
                 recv_sem=recv_a.at[0, k],
-                device_id=place(my_b, a),
+                device_id=other,
                 device_id_type=MESH,
             )
         )
@@ -284,7 +308,25 @@
     resp_send[...] = jnp.dot(sel[...], gathered[...], preferred_element_type=F32).astype(BF16)
     answers = exchange_b(1, resp_send, resp_recv)
 
-    sel_t[...] = jnp.transpose(sel[...].astype(F32)).astype(BF16)
+    sel_t = jnp.transpose(sel[...].astype(F32)).astype(BF16)
+    slot = iota((slots, 128), 0)
+    fold = jnp.where(slot // per * 2 + lax.rem(slot, 2) == iota((slots, 128), 1), 1.0, 0.0)
+    route_send[...] = jnp.dot(sel_t, fold.astype(BF16), preferred_element_type=F32).astype(BF16)
+    routes = []
+    for k, (a, other) in enumerate(partners_a):
+        routes.append(
+            pltpu.make_async_remote_copy(
+                src_ref=route_send.at[pl.ds(pl.multiple_of(a * blocks, blocks), blocks)],
+                dst_ref=route_recv.at[my_rows],
+                send_sem=send_a.at[1, k],
+                recv_sem=recv_a.at[1, k],
+                device_id=other,
+                device_id_type=MESH,
+            )
+        )
+    for item in routes:
+        item.start()
+    route_recv[my_rows, :] = route_send[my_rows, :]
 
     for item in loads[9:12]:
         item.wait()
@@ -338,7 +380,26 @@
     img_send[...] = jnp.dot(
         slot_hot[...], image[...].astype(BF16), preferred_element_type=F32
     ).astype(BF16)
-    images = exchange_b(2, img_send, img_recv)
+    images = []
+    for owner, relay, other in partners:
+        images.append(
+            pltpu.make_async_remote_copy(
+                src_ref=img_send.at[pl.ds(owner * 2, 2)],
+                dst_ref=img_recv.at[pl.ds((relay * gb + my_b) * 2, 2)],
+                send_sem=img_sem.at[0],
+                recv_sem=img_sem.at[1],
+                device_id=other,
+                device_id_type=MESH,
+            )
+        )
+    for item in images:
+        item.start()
+    own_image = pltpu.make_async_copy(
+        img_send.at[pl.ds((my_b * ga + my_a) * 2, 2)],
+        img_recv.at[pl.ds((my_a * gb + my_b) * 2, 2)],
+        img_sem.at[2],
+    )
+    own_image.start()
     loads[12].wait()
 
     @pl.loop(0, blocks // 2)
@@ -351,31 +412,15 @@
         pre_high[:, lanes] = upper
         pre_low[:, lanes] = (both - upper.astype(F32)).astype(BF16)
 
-    for item in images:
+    for item in routes:
         item.wait_recv()
-
-    sum_send[...] = jnp.dot(sel_t[...], img_recv[...], preferred_element_type=F32).astype(BF16)
-    sums = []
-    for k, a in enumerate(partners_a):
-        sums.append(
-            pltpu.make_async_remote_copy(
-                src_ref=sum_send.at[pl.ds(pl.multiple_of(a * blocks, blocks), blocks)],
-                dst_ref=sum_recv.at[my_rows],
-                send_sem=send_a.at[1, k],
-                recv_sem=recv_a.at[1, k],
-                device_id=place(my_b, a),
-                device_id_type=MESH,
-            )
-        )
-    for item in sums:
-        item.start()
-    sum_recv[my_rows, :] = sum_send[my_rows, :]
-    for item in sums:
-        item.wait_recv()
-
-    total = inner[...]
-    for a in range(ga):
-        total = total + sum_recv[a * blocks : (a + 1) * blocks, :].astype(F32)
+    route = jnp.concatenate(
+        [route_recv[a * blocks : (a + 1) * blocks, 0 : 2 * gb] for a in range(ga)], axis=1
+    )
+    own_image.wait()
+    others = pl.ds(0, slots - 2)
+    pltpu.make_async_copy(img_recv.at[others], img_recv.at[others], img_sem.at[1]).wait()
+    total = inner[...] + jnp.dot(route, img_recv[...], preferred_element_type=F32)
     width = 8 * nodes
     keep = iota((8, width), 1) // nodes == iota((8, width), 0)
     for at in range(0, blocks, 8):
@@ -393,13 +438,14 @@
         out[0, at : at + 8, :] = result[0:8] + result[8:16]
         out[1, at : at + 8, :] = result[16:24] + result[24:32]
 
-    for item in requests + tables + answers + images + sums:
+    for item in requests + tables + answers + routes:
         item.wait_send()
+    pltpu.make_async_copy(img_send.at[others], img_send.at[others], img_sem.at[0]).wait()
 
 
 def solution(mesh):
     devices = mesh.shape["dom"] * mesh.shape["sub"]
-    ga = min(GROUP_A, devices // 2)
+    ga = GROUP_A
     gb = devices // ga
 
     def per_device(*arrays):
@@ -446,7 +492,6 @@
             vmem((slots, 128), BF16),
             vmem((slots, 128), BF16),
             vmem((slots, wide), BF16),
-            vmem((wide, slots), BF16),
             vmem((slots, 128), BF16),
             vmem((slots, 128), BF16),
             vmem((slots, 128), BF16),
@@ -454,10 +499,11 @@
             vmem((wide, 128), BF16),
             vmem((wide, 128), BF16),
             pltpu.SemaphoreType.DMA((len(given),)),
-            pltpu.SemaphoreType.DMA((3, gb - 1)),
-            pltpu.SemaphoreType.DMA((3, gb - 1)),
+            pltpu.SemaphoreType.DMA((2, gb - 1)),
+            pltpu.SemaphoreType.DMA((2, gb - 1)),
             pltpu.SemaphoreType.DMA((2, ga - 1)),
             pltpu.SemaphoreType.DMA((2, ga - 1)),
+            pltpu.SemaphoreType.DMA((3,)),
         ]
         result = pl.pallas_call(
             functools.partial(body, (ga, gb, blocks, stamps, nodes, elements)),

time: 31.3 us -> 27.9 us (0.89)
  Pallas kernels: 29.7 us -> 26.3 us
    pallas_call x1, Pallas kernels: 29.7 us -> 26.3 us  [per_device(): pl.pallas_call(functools.partial(body, (ga, gb, blocks, stamps, nodes, el...]
where the time goes in v3:
time: 27.9 us; the launch traced here: 27.7 us
  Pallas kernels  26.3 us (94%)
  local copies, waits for them, and re-layouts  1.38 us (5%)
    pallas_call x1, Pallas kernels, per_device(): pl.pallas_call(functools.partial(body, (ga, gb, blocks, stamps, nodes, el...  26.3 us
    unnamed x1, local copies, waits for them, and re-layouts  1.38 us

profile of v3, /device:TPU:1, one launch (start us, length us, event | category | flops | bytes accessed | tf_op | source)
XLA Modules:
  0.0 27.7 jit_solution(11056237675231270485)
XLA Ops:
  0.0 26.3 %shard_map.127 = f32[2,32,64]{2,1,0:T(8,128)} custom-call(f32[32,64]{1,0:T(8,128)} %bitcast.13, f32[2,32,64]{2,1,0:T(8,128)} %bitcast.12, f32[32,64]{1,0:T(8,128)} %bitcast.14, f32[2048,64]{1,0:T(8,128)} %bitcast.10, s32[1,64]{1,0:T(1,128)} %bitcast.15, s32[1,64]{1,0:T(1,128)} %bitcast.16, s32[1,64]{1,0:T(1,128)} %bitcast.17, s32[64,768]{1,0:T(8,128)} %csrc_h.1, ...), custom_call_target="tpu_custom_call" | custom-call | tf_op jit(solution)/shard_map/pallas_call | solution.py:508
  26.4 1.4 %copy.15 = f32[2,64,32]{1,2,0:T(8,128)} copy(f32[2,64,32]{1,2,0:T(8,128)} %bitcast.11) | data formatting | bytes 32768

commit v4 on v3

--- a/solution.py
+++ b/solution.py
@@ -135,21 +135,20 @@
     def hops(dz, dq, dy):
         return sum(min(d % 4, -d % 4) for d in (dz, dy, dq + 2 * dy))
 
-    partners_a = []
-    for k in range(1, ga):
-        a = lax.rem(my_a + k, ga)
-        partners_a.append((a, place(my_z, my_q, a // 2, lax.rem(a, 2))))
-    partners_b, partners = [], []
     steps = [(dz, dq, dy, dc) for dz in range(gb // 4) for dq in range(4) for dy in range(4) for dc in range(2)]
-    for dz, dq, dy, dc in sorted(steps, key=lambda d: -hops(*d[:3])):
-        if (dz, dq, dy, dc) == (0, 0, 0, 0):
-            continue
+    steps = [step for step in sorted(steps, key=lambda d: -hops(*d[:3])) if any(step)]
+    partners_a, partners_b = [], []
+    for dz, dq, dy, dc in steps:
         z, q = lax.rem(my_z + dz, gb // 4), lax.rem(my_q + dq, 4)
         y, c = lax.rem(my_y + dy, 4), lax.rem(core + dc, 2)
-        relay = (flipped if dq == 2 else my_y) * 2 + core
-        partners.append(((z * 4 + q) * ga + y * 2 + c, relay, place(z, q, y, c)))
-        if dc == 0 and dy == (1 if dq == 2 else 0):
+        if dz == 0 and dq == 0:
+            partners_a.append((y * 2 + c, place(z, q, y, c)))
+        elif dc == 0 and dy == (1 if dq == 2 else 0):
             partners_b.append((z * 4 + q, place(z, q, flipped if dq == 2 else my_y, core)))
+
+    barrier = pltpu.get_barrier_semaphore()
+    for _, other in partners_b + partners_a:
+        pl.semaphore_signal(barrier, inc=1, device_id=other, device_id_type=MESH)
 
     pairs = [
         (cown_h, cown),
@@ -170,10 +169,6 @@
     for item in loads:
         item.start()
 
-    barrier = pltpu.get_barrier_semaphore()
-    for _, other in partners_b + partners_a:
-        pl.semaphore_signal(barrier, inc=1, device_id=other, device_id_type=MESH)
-
     for item in loads[:6]:
         item.wait()
 
@@ -219,15 +214,21 @@
 
     pl.semaphore_wait(barrier, ga + gb - 2)
 
+    def wait_all(ref, rows, sem):
+        whole = ref.at[pl.ds(0, rows)]
+        pltpu.make_async_copy(whole, whole, sem).wait()
+
+    others_b, others_a = (gb - 1) * per, (ga - 1) * blocks
+
     def exchange_b(phase, source, target):
         copies = []
-        for k, (b, other) in enumerate(partners_b):
+        for b, other in partners_b:
             copies.append(
                 pltpu.make_async_remote_copy(
                     src_ref=source.at[pl.ds(pl.multiple_of(b * per, per), per)],
                     dst_ref=target.at[pl.ds(pl.multiple_of(my_b * per, per), per)],
-                    send_sem=send_b.at[phase, k],
-                    recv_sem=recv_b.at[phase, k],
+                    send_sem=send_b.at[phase],
+                    recv_sem=recv_b.at[phase],
                     device_id=other,
                     device_id_type=MESH,
                 )
@@ -236,17 +237,16 @@
             item.start()
         mine = pl.ds(pl.multiple_of(my_b * per, per), per)
         target[mine, :] = source[mine, :]
-        return copies
-
-    requests = exchange_b(0, req_send, req_recv)
+
+    exchange_b(0, req_send, req_recv)
     tables = []
-    for k, (a, other) in enumerate(partners_a):
+    for a, other in partners_a:
         tables.append(
             pltpu.make_async_remote_copy(
                 src_ref=gathered.at[my_rows],
                 dst_ref=gathered.at[my_rows],
-                send_sem=send_a.at[0, k],
-                recv_sem=recv_a.at[0, k],
+                send_sem=send_a.at[0],
+                recv_sem=recv_a.at[0],
                 device_id=other,
                 device_id_type=MESH,
             )
@@ -294,10 +294,8 @@
         cap_here = cap[rows, :]
         inner[rows, :] = spread + jnp.concatenate([cap_here, cap_here], axis=1) * upd
 
-    for item in requests:
-        item.wait_recv()
-    for item in tables:
-        item.wait_recv()
+    wait_all(req_recv, others_b, recv_b.at[0])
+    wait_all(gathered, others_a, recv_a.at[0])
 
     asked_here = req_recv[...].astype(F32)
     wide = ga * blocks
@@ -306,20 +304,20 @@
         lane = (iota((slots, width), 1) + at).astype(F32)
         sel[:, at : at + width] = jnp.where(asked_here[:, 0:width] == lane, 1.0, 0.0).astype(BF16)
     resp_send[...] = jnp.dot(sel[...], gathered[...], preferred_element_type=F32).astype(BF16)
-    answers = exchange_b(1, resp_send, resp_recv)
+    exchange_b(1, resp_send, resp_recv)
 
     sel_t = jnp.transpose(sel[...].astype(F32)).astype(BF16)
     slot = iota((slots, 128), 0)
     fold = jnp.where(slot // per * 2 + lax.rem(slot, 2) == iota((slots, 128), 1), 1.0, 0.0)
     route_send[...] = jnp.dot(sel_t, fold.astype(BF16), preferred_element_type=F32).astype(BF16)
     routes = []
-    for k, (a, other) in enumerate(partners_a):
+    for a, other in partners_a:
         routes.append(
             pltpu.make_async_remote_copy(
                 src_ref=route_send.at[pl.ds(pl.multiple_of(a * blocks, blocks), blocks)],
                 dst_ref=route_recv.at[my_rows],
-                send_sem=send_a.at[1, k],
-                recv_sem=recv_a.at[1, k],
+                send_sem=send_a.at[1],
+                recv_sem=recv_a.at[1],
                 device_id=other,
                 device_id_type=MESH,
             )
@@ -348,8 +346,7 @@
                 spread == node[0:DIGIT], one[0:DIGIT], none[0:DIGIT]
             )
 
-    for item in answers:
-        item.wait_recv()
+    wait_all(resp_recv, others_b, recv_b.at[1])
     far_table[...] = jnp.dot(slot_hot_t[...], resp_recv[...], preferred_element_type=F32)
 
     @pl.loop(0, stamps // 8, unroll=True)
@@ -381,14 +378,18 @@
         slot_hot[...], image[...].astype(BF16), preferred_element_type=F32
     ).astype(BF16)
     images = []
-    for owner, relay, other in partners:
+    for dz, dq, dy, dc in steps:
+        z, q = lax.rem(my_z + dz, gb // 4), lax.rem(my_q + dq, 4)
+        y, c = lax.rem(my_y + dy, 4), lax.rem(core + dc, 2)
+        owner = (z * 4 + q) * ga + y * 2 + c
+        relay = (flipped if dq == 2 else my_y) * 2 + core
         images.append(
             pltpu.make_async_remote_copy(
                 src_ref=img_send.at[pl.ds(owner * 2, 2)],
                 dst_ref=img_recv.at[pl.ds((relay * gb + my_b) * 2, 2)],
                 send_sem=img_sem.at[0],
                 recv_sem=img_sem.at[1],
-                device_id=other,
+                device_id=place(z, q, y, c),
                 device_id_type=MESH,
             )
         )
@@ -412,14 +413,12 @@
         pre_high[:, lanes] = upper
         pre_low[:, lanes] = (both - upper.astype(F32)).astype(BF16)
 
-    for item in routes:
-        item.wait_recv()
+    wait_all(route_recv, others_a, recv_a.at[1])
     route = jnp.concatenate(
         [route_recv[a * blocks : (a + 1) * blocks, 0 : 2 * gb] for a in range(ga)], axis=1
     )
     own_image.wait()
-    others = pl.ds(0, slots - 2)
-    pltpu.make_async_copy(img_recv.at[others], img_recv.at[others], img_sem.at[1]).wait()
+    wait_all(img_recv, slots - 2, img_sem.at[1])
     total = inner[...] + jnp.dot(route, img_recv[...], preferred_element_type=F32)
     width = 8 * nodes
     keep = iota((8, width), 1) // nodes == iota((8, width), 0)
@@ -438,9 +437,11 @@
         out[0, at : at + 8, :] = result[0:8] + result[8:16]
         out[1, at : at + 8, :] = result[16:24] + result[24:32]
 
-    for item in requests + tables + answers + routes:
-        item.wait_send()
-    pltpu.make_async_copy(img_send.at[others], img_send.at[others], img_sem.at[0]).wait()
+    wait_all(req_send, others_b, send_b.at[0])
+    wait_all(gathered, others_a, send_a.at[0])
+    wait_all(resp_send, others_b, send_b.at[1])
+    wait_all(route_send, others_a, send_a.at[1])
+    wait_all(img_send, slots - 2, img_sem.at[0])
 
 
 def solution(mesh):
@@ -499,20 +500,20 @@
             vmem((wide, 128), BF16),
             vmem((wide, 128), BF16),
             pltpu.SemaphoreType.DMA((len(given),)),
-            pltpu.SemaphoreType.DMA((2, gb - 1)),
-            pltpu.SemaphoreType.DMA((2, gb - 1)),
-            pltpu.SemaphoreType.DMA((2, ga - 1)),
-            pltpu.SemaphoreType.DMA((2, ga - 1)),
+            pltpu.SemaphoreType.DMA((2,)),
+            pltpu.SemaphoreType.DMA((2,)),
+            pltpu.SemaphoreType.DMA((2,)),
+            pltpu.SemaphoreType.DMA((2,)),
             pltpu.SemaphoreType.DMA((3,)),
         ]
         result = pl.pallas_call(
             functools.partial(body, (ga, gb, blocks, stamps, nodes, elements)),
-            out_shape=jax.ShapeDtypeStruct((2, blocks, nodes), F32),
+            out_shape=pltpu.VMEM((2, blocks, nodes), F32),
             in_specs=[pl.BlockSpec(memory_space=pl.ANY)] * len(given),
             out_specs=pl.BlockSpec(memory_space=pltpu.VMEM),
             scratch_shapes=scratch,
             compiler_params=pltpu.CompilerParams(
-                collective_id=0, has_side_effects=True, vmem_limit_bytes=67043328
+                collective_id=0, has_side_effects=True, vmem_limit_bytes=66_000_000
             ),
         )(*given)
         return result.transpose(0, 2, 1)

time: 27.9 us -> 25.6 us (0.918)
  Pallas kernels: 26.3 us -> 24.9 us
  local copies, waits for them, and re-layouts: 1.38 us -> 0.62 us
    pallas_call x1, Pallas kernels: 26.3 us -> 24.9 us  [per_device(): pl.pallas_call(functools.partial(body, (ga, gb, blocks, stamps, nodes, el...]
    unnamed x1, local copies, waits for them, and re-layouts: 1.38 us -> 0.62 us
where the time goes in v4:
time: 25.6 us; the launch traced here: 25.5 us
  Pallas kernels  24.9 us (97%)
  local copies, waits for them, and re-layouts  0.62 us (2%)
    pallas_call x1, Pallas kernels, per_device(): pl.pallas_call(functools.partial(body, (ga, gb, blocks, stamps, nodes, el...  24.9 us
    unnamed x1, local copies, waits for them, and re-layouts  0.62 us

profile of v4, /device:TPU:1, one launch (start us, length us, event | category | flops | bytes accessed | tf_op | source)
XLA Modules:
  0.0 25.5 jit_solution(7789637980768061763)
XLA Ops:
  0.0 24.9 %shard_map.127 = f32[2,32,64]{2,1,0:T(8,128)S(1)} custom-call(f32[32,64]{1,0:T(8,128)} %bitcast.13, f32[2,32,64]{2,1,0:T(8,128)} %bitcast.12, f32[32,64]{1,0:T(8,128)} %bitcast.14, f32[2048,64]{1,0:T(8,128)} %bitcast.11, s32[1,64]{1,0:T(1,128)} %bitcast.15, s32[1,64]{1,0:T(1,128)} %bitcast.16, s32[1,64]{1,0:T(1,128)} %bitcast.17, s32[64,768]{1,0:T(8,128)} %csrc_h.1, ...), custom_call_target="tpu_custom_call" | custom-call | tf_op jit(solution)/shard_map/pallas_call | solution.py:509
  24.9 0.6 %copy.15 = f32[2,64,32]{1,2,0:T(8,128)} copy(f32[2,64,32]{1,2,0:T(8,128)S(1)} %bitcast.10) | data formatting | bytes 32768

commit v5 on v4

--- a/solution.py
+++ b/solution.py
@@ -95,8 +95,7 @@
     inner,
     hot,
     hot_inner,
-    pre_high,
-    pre_low,
+    pre_t,
     near0,
     near1,
     upd0,
@@ -238,7 +237,6 @@
         mine = pl.ds(pl.multiple_of(my_b * per, per), per)
         target[mine, :] = source[mine, :]
 
-    exchange_b(0, req_send, req_recv)
     tables = []
     for a, other in partners_a:
         tables.append(
@@ -253,6 +251,8 @@
         )
     for item in tables:
         item.start()
+
+    exchange_b(0, req_send, req_recv)
 
     blk_hot = jnp.where(
         iota((stamps, blocks), 1).astype(F32) == column(cblk[...].astype(F32)), 1.0, 0.0
@@ -295,7 +295,6 @@
         inner[rows, :] = spread + jnp.concatenate([cap_here, cap_here], axis=1) * upd
 
     wait_all(req_recv, others_b, recv_b.at[0])
-    wait_all(gathered, others_a, recv_a.at[0])
 
     asked_here = req_recv[...].astype(F32)
     wide = ga * blocks
@@ -303,6 +302,7 @@
         width = min(128, wide - at)
         lane = (iota((slots, width), 1) + at).astype(F32)
         sel[:, at : at + width] = jnp.where(asked_here[:, 0:width] == lane, 1.0, 0.0).astype(BF16)
+    wait_all(gathered, others_a, recv_a.at[0])
     resp_send[...] = jnp.dot(sel[...], gathered[...], preferred_element_type=F32).astype(BF16)
     exchange_b(1, resp_send, resp_recv)
 
@@ -329,6 +329,11 @@
     for item in loads[9:12]:
         item.wait()
 
+    seats = jnp.where(
+        iota((8, 8 * DIGIT), 1) // DIGIT == iota((8, 8 * DIGIT), 0), 1.0, 0.0
+    ).astype(BF16)
+    digit = (iota((elements, 8 * DIGIT), 1) & (DIGIT - 1)).astype(F32)
+
     @pl.loop(0, stamps // 8)
     def _(g):
         rows = pl.ds(pl.multiple_of(g * 8, 8), 8)
@@ -338,13 +343,10 @@
         near1[rows, :] = lookup(tab, first + nodes)
         upd0[rows, :] = lookup(upd, first)
         upd1[rows, :] = lookup(upd, first + nodes)
-        low = second & (DIGIT - 1)
-        base = g * (8 * DIGIT)
-        for r in range(8):
-            spread = jnp.broadcast_to(low[r : r + 1, :].astype(F32), (DIGIT, elements)).astype(BF16)
-            hot[pl.ds(pl.multiple_of(base + r * DIGIT, DIGIT), DIGIT), :] = jnp.where(
-                spread == node[0:DIGIT], one[0:DIGIT], none[0:DIGIT]
-            )
+        low = (second & (DIGIT - 1)).astype(F32).astype(BF16)
+        low = lax.dot_general(low, seats, (((0,), (0,)), ((), ())), preferred_element_type=F32)
+        here = pl.ds(pl.multiple_of(g * elements, elements), elements)
+        hot[here, :] = jnp.where(low == digit, 1.0, 0.0).astype(BF16)
 
     wait_all(resp_recv, others_b, recv_b.at[1])
     far_table[...] = jnp.dot(slot_hot_t[...], resp_recv[...], preferred_element_type=F32)
@@ -356,21 +358,19 @@
         tab = far_table[rows, :]
         w0 = -conductance(gain, near0[rows, :], lookup(tab, second)) * upd0[rows, :]
         w1 = -conductance(gain, near1[rows, :], lookup(tab, second + nodes)) * upd1[rows, :]
-        mine = hot[pl.ds(pl.multiple_of(g * (8 * DIGIT), 8 * DIGIT), 8 * DIGIT), :]
+        mine = hot[pl.ds(pl.multiple_of(g * elements, elements), elements), :]
         high = lax.shift_right_logical(second, DIGIT.bit_length() - 1)
-        parts = []
-        for item in (w0, w1):
-            upper = item.astype(BF16).astype(F32)
-            parts += [upper, item - upper]
-        left = [jnp.where(high == h, item, 0.0) for h in range(nodes // DIGIT) for item in parts]
-        spread = nt_dot(jnp.concatenate(left, axis=0).astype(BF16), mine)
+        left = [jnp.where(high == h, w, 0.0) for h in range(nodes // DIGIT) for w in (w0, w1)]
+        spread = jnp.dot(
+            jnp.concatenate(left, axis=0).astype(BF16), mine, preferred_element_type=F32
+        )
         lane = iota((8, 128), 1)
         pick = iota((8, 128), 0) * DIGIT + (lane & (DIGIT - 1))
         total = jnp.zeros((8, 128), F32)
         for h in range(nodes // DIGIT):
             for t in range(2):
-                at = (h * 4 + t * 2) * 8
-                piece = lookup(spread[at : at + 8] + spread[at + 8 : at + 16], pick)
+                at = (h * 2 + t) * 8
+                piece = lookup(spread[at : at + 8], pick)
                 total = jnp.where(lane // DIGIT == t * (nodes // DIGIT) + h, piece, total)
         image[rows, :] = total
 
@@ -408,10 +408,9 @@
         both = jnp.concatenate(
             [pre[pl.ds(2 * c + n, nodes, stride=blocks), :] for n in range(2)], axis=1
         )
-        upper = both.astype(BF16)
-        lanes = pl.ds(pl.multiple_of(c * 128, 128), 128)
-        pre_high[:, lanes] = upper
-        pre_low[:, lanes] = (both - upper.astype(F32)).astype(BF16)
+        upper = both.astype(BF16).astype(F32)
+        parts = jnp.concatenate([upper, both - upper], axis=0)
+        pre_t[pl.ds(pl.multiple_of(c * 128, 128), 128), :] = jnp.transpose(parts).astype(BF16)
 
     wait_all(route_recv, others_a, recv_a.at[1])
     route = jnp.concatenate(
@@ -432,10 +431,12 @@
                 for item in (jnp.where(low_half, here, turned), jnp.where(low_half, turned, here))
             )
         )
-        lanes = slice(at * nodes, (at + 8) * nodes)
-        result = nt_dot(left, pre_high[:, lanes]) + nt_dot(left, pre_low[:, lanes])
-        out[0, at : at + 8, :] = result[0:8] + result[8:16]
-        out[1, at : at + 8, :] = result[16:24] + result[24:32]
+        result = jnp.dot(
+            left, pre_t[at * nodes : (at + 8) * nodes, :], preferred_element_type=F32
+        )
+        for t in range(2):
+            both = result[16 * t : 16 * t + 8] + result[16 * t + 8 : 16 * t + 16]
+            out[t, at : at + 8, :] = (both + pltpu.roll(both, nodes, 1))[:, 0:nodes]
 
     wait_all(req_send, others_b, send_b.at[0])
     wait_all(gathered, others_a, send_a.at[0])
@@ -479,10 +480,9 @@
             vmem((stamps, 128), F32),
             vmem((stamps, 128), F32),
             vmem((blocks, 128), F32),
-            vmem((stamps * DIGIT, elements), BF16),
+            vmem((stamps // 8 * elements, 8 * DIGIT), BF16),
             vmem((8 * nodes, elements), BF16),
-            vmem((nodes, blocks * nodes), BF16),
-            vmem((nodes, blocks * nodes), BF16),
+            vmem((blocks * nodes, 128), BF16),
             vmem((stamps, elements), F32),
             vmem((stamps, elements), F32),
             vmem((stamps, elements), F32),

time: 25.6 us -> 25.4 us (level)
  no operation moved by 1% of the time
where the time goes in v5:
time: 25.4 us; the launch traced here: 25.3 us
  Pallas kernels  24.7 us (97%)
  local copies, waits for them, and re-layouts  0.62 us (2%)
    pallas_call x1, Pallas kernels, per_device(): pl.pallas_call(functools.partial(body, (ga, gb, blocks, stamps, nodes, el...  24.7 us
    unnamed x1, local copies, waits for them, and re-layouts  0.62 us

profile of v5, /device:TPU:1, one launch (start us, length us, event | category | flops | bytes accessed | tf_op | source)
XLA Modules:
  0.0 25.3 jit_solution(10207531823562952261)
XLA Ops:
  0.0 24.7 %shard_map.127 = f32[2,32,64]{2,1,0:T(8,128)S(1)} custom-call(f32[32,64]{1,0:T(8,128)} %bitcast.13, f32[2,32,64]{2,1,0:T(8,128)} %bitcast.12, f32[32,64]{1,0:T(8,128)} %bitcast.14, f32[2048,64]{1,0:T(8,128)} %bitcast.11, s32[1,64]{1,0:T(1,128)} %bitcast.15, s32[1,64]{1,0:T(1,128)} %bitcast.16, s32[1,64]{1,0:T(1,128)} %bitcast.17, s32[64,768]{1,0:T(8,128)} %csrc_h.1, ...), custom_call_target="tpu_custom_call" | custom-call | tf_op jit(solution)/shard_map/pallas_call | solution.py:509
  24.7 0.6 %copy.15 = f32[2,64,32]{1,2,0:T(8,128)} copy(f32[2,64,32]{1,2,0:T(8,128)S(1)} %bitcast.10) | data formatting | bytes 32768
